TPU v7x, 256 devices: a whole 4x4x8 slice. The times are simulated.
256 devices in a mesh: region: 32 (over x, z), group: 8 (over y, core).
Axes of the slice: x: 4, y: 4, z: 8, core: 2. Of those that a mesh axis runs over, the one named last changes fastest.
Arguments:
- block_coords: int32 [8, 192, 3], P('group', 'region'), may hold values from -100 to 63, as said below
- features: bfloat16 [8, 192, 8, 8, 8, 128], P('group', 'region'), may hold values from -6 to 6
- cotangent: bfloat16 [8, 192, 4, 4, 4, 128], P('group', 'region'), may hold values from -6 to 6
- weights: bfloat16 [3, 3, 3, 128, 128], replicated, may hold values from -0.109375 to 0.109375
Outputs:
- coarse_features: bfloat16 [8, 192, 4, 4, 4, 128], P('group', 'region')
- grad_features: bfloat16 [8, 192, 8, 8, 8, 128], P('group', 'region')
- grad_weight: float32 [3, 3, 3, 128, 128], replicated
Inputs may be any that keep to these rules, and one draw needn't show every extreme that they name: `block_coords`: slot s of device r along region holds a block with coordinates (x, y, z), x being 2r or 2r+1, 0 <= y < 1, 0 <= z < 4; a device's blocks are distinct; its occupied slots come first and the others hold -100 in all three coordinates; every device holds 3 to 6 blocks, and in each map one device holds 6 and another 6 // 2.
All inputs are finite; a program needn't handle non-finite values.
Results may differ from a plain program's by a relative error of at most 0.0023.
Values may be sent and summed in bfloat16 or wider, within the bound.
No kernel may reach another device: no remote copies, remote signals or barrier semaphores. Data moves between devices by JAX's collectives and lax.ppermute only.
A program may use at most 64 MiB of HBM per device.

v0:
```python
import math
import jax
import jax.numpy as jnp
from jax import lax
from jax.sharding import PartitionSpec as P

CROSS_Y = 1
CROSS_Z = 4
LOWER_SIDES = (
    (-1, 0, 0),
    (-1, -1, 0),
    (-1, 0, -1),
    (-1, -1, -1),
    (0, -1, 0),
    (0, 0, -1),
    (0, -1, -1),
)


def shifted(block, axis, distance):
    devices = range(lax.axis_size(axis))
    route = [(i - distance, i) for i in devices if i - distance in devices]
    return lax.ppermute(block, axis, route)


def unfold(volume, which_axis):
    pieces = [lax.slice_in_dim(volume, offset, offset + 7, 2, which_axis) for offset in range(3)]
    return jnp.stack(pieces, axis=which_axis + 1)


def fold_back(col_terms, which_axis):
    lower_part, middle_part, upper_part = [
        lax.index_in_dim(col_terms, offset, which_axis + 1, keepdims=False) for offset in range(3)
    ]
    zero_row = jnp.zeros_like(lax.slice_in_dim(lower_part, 0, 1, 1, which_axis))
    even_rows = jnp.concatenate([lower_part, zero_row], which_axis) + jnp.concatenate(
        [zero_row, upper_part], which_axis
    )
    paired = jnp.stack(
        [lax.slice_in_dim(even_rows, 0, 4, 1, which_axis), middle_part], which_axis + 1
    )
    new_shape = list(lower_part.shape)
    new_shape[which_axis] = 8
    merged = paired.reshape(new_shape)
    return jnp.concatenate([merged, lax.slice_in_dim(even_rows, 4, 5, 1, which_axis)], which_axis)


def pick_rows(lookup_table, link):
    safe_rows = jnp.clip(link[0], 0, lookup_table.shape[0] - 1)
    gathered = jnp.take(lookup_table, safe_rows, axis=0)
    present_mask = link[1].reshape((-1,) + (1,) * (gathered.ndim - 1))
    return jnp.where(present_mask, gathered, jnp.zeros_like(gathered))


def assemble(blocks, planes, source_links):
    face_x = pick_rows(planes, source_links[0])
    edge_xy = pick_rows(planes[:, 7], source_links[1])
    edge_xz = pick_rows(planes[:, :, 7], source_links[2])
    corner = pick_rows(planes[:, 7, 7], source_links[3])
    face_y = pick_rows(blocks[:, :, 7], source_links[4])
    face_z = pick_rows(blocks[:, :, :, 7], source_links[5])
    edge_yz = pick_rows(blocks[:, :, 7, 7], source_links[6])
    first_plane = jnp.concatenate(
        [
            jnp.concatenate([corner[:, None, None], edge_xy[:, None]], axis=2),
            jnp.concatenate([edge_xz[:, :, None], face_x], axis=2),
        ],
        axis=1,
    )
    low_row = jnp.concatenate([edge_yz[:, :, None], face_y], axis=2)[:, :, None]
    interior = jnp.concatenate([face_z[:, :, :, None], blocks], axis=3)
    upper_part = jnp.concatenate([low_row, interior], axis=2)
    return jnp.concatenate([first_plane[:, None], upper_part], axis=1)


def aim_rows(link, limit):
    return jnp.where(link[1], link[0], limit)


def spread_rims(ext_grads, source_links, block_count, table_rows):
    own_grad = ext_grads[:, 1:, 1:, 1:]
    planes = jnp.zeros((table_rows,) + own_grad.shape[2:], ext_grads.dtype)
    planes = planes.at[aim_rows(source_links[0], table_rows)].add(
        ext_grads[:, 0, 1:, 1:], mode="drop"
    )
    planes = planes.at[aim_rows(source_links[1], table_rows), 7].add(
        ext_grads[:, 0, 0, 1:], mode="drop"
    )
    planes = planes.at[aim_rows(source_links[2], table_rows), :, 7].add(
        ext_grads[:, 0, 1:, 0], mode="drop"
    )
    planes = planes.at[aim_rows(source_links[3], table_rows), 7, 7].add(
        ext_grads[:, 0, 0, 0], mode="drop"
    )
    own_grad = own_grad.at[aim_rows(source_links[4], block_count), :, 7].add(
        ext_grads[:, 1:, 0, 1:], mode="drop"
    )
    own_grad = own_grad.at[aim_rows(source_links[5], block_count), :, :, 7].add(
        ext_grads[:, 1:, 1:, 0], mode="drop"
    )
    own_grad = own_grad.at[aim_rows(source_links[6], block_count), :, 7, 7].add(
        ext_grads[:, 1:, 0, 0], mode="drop"
    )
    return (own_grad, planes)


def find_links(coords, region_rank, block_count):
    slot_ids = jnp.arange(block_count, dtype=jnp.int32)
    collected = []
    for side in LOWER_SIDES:
        wanted = coords + jnp.array(side, jnp.int32)
        matches = jnp.all(wanted[:, None, :] == coords[None, :, :], axis=2)
        present = jnp.any(matches, axis=1)
        source = jnp.sum(jnp.where(matches, slot_ids[None, :], 0), axis=1)
        if side[0] == -1:
            remote = (
                (wanted[:, 0] == 2 * region_rank - 1)
                & (wanted[:, 1] >= 0)
                & (wanted[:, 1] < CROSS_Y)
                & (wanted[:, 2] >= 0)
                & (wanted[:, 2] < CROSS_Z)
            )
            source = jnp.where(present, source, block_count + wanted[:, 1] * CROSS_Z + wanted[:, 2])
            present = present | remote
        collected.append((source, present))
    return collected


def per_device(block_coords, features, cotangent, weights):
    coords = block_coords[0]
    blocks = features[0]
    upstream = cotangent[0]
    block_count = blocks.shape[0]
    cell_count = CROSS_Y * CROSS_Z
    region_rank = lax.axis_index("region")
    occupied = coords[:, 0] >= 0
    cell_index = coords[:, 1] * CROSS_Z + coords[:, 2]
    in_top = coords[:, 0] == 2 * region_rank + 1
    top_planes = blocks[:, 7]
    outgoing = (
        jnp.zeros((cell_count,) + top_planes.shape[1:], blocks.dtype)
        .at[jnp.where(in_top, cell_index, cell_count)]
        .set(top_planes, mode="drop")
    )
    incoming = shifted(outgoing, "region", 1)
    source_links = find_links(coords, region_rank, block_count)
    plane_table = jnp.concatenate([top_planes, incoming], axis=0)
    extended = assemble(blocks, plane_table, source_links)
    columns = unfold(unfold(unfold(extended, 1), 3), 5)
    block_mask = occupied[:, None, None, None, None]
    result = jnp.einsum(
        "nxaybzcf,abcfo->nxyzo", columns, weights, preferred_element_type=jnp.float32
    )
    coarse = jnp.where(block_mask, result, 0.0).astype(jnp.bfloat16)
    masked = jnp.where(block_mask, upstream, jnp.zeros_like(upstream))
    local_grad = jnp.einsum(
        "nxaybzcf,nxyzo->abcfo", columns, masked, preferred_element_type=jnp.float32
    )
    col_terms = jnp.einsum(
        "nxyzo,abcfo->nxaybzcf", masked, weights, preferred_element_type=jnp.float32
    )
    ext_grads = fold_back(fold_back(fold_back(col_terms, 5), 3), 1)
    own_grad, plane_grads = spread_rims(
        ext_grads, source_links, block_count, block_count + cell_count
    )
    own_grad = own_grad.at[:, 7].add(plane_grads[:block_count])
    returned = shifted(plane_grads[block_count:].astype(jnp.bfloat16), "region", -1).astype(
        jnp.float32
    )
    own_grad = own_grad.at[:, 7].add(pick_rows(returned, (cell_index, in_top)))
    summed = lax.psum(local_grad, ("region", "group"))
    grad_scale = 1.0 / math.sqrt(
        lax.axis_size("group") * lax.axis_size("region") * block_count * upstream.shape[1] ** 3
    )
    return (coarse[None], own_grad.astype(jnp.bfloat16)[None], summed * grad_scale)


def solution(mesh):
    return jax.shard_map(
        per_device,
        mesh=mesh,
        in_specs=(
            P("group", "region", None),
            P("group", "region", None, None, None, None),
            P("group", "region", None, None, None, None),
            P(),
        ),
        out_specs=(
            P("group", "region", None, None, None, None),
            P("group", "region", None, None, None, None),
            P(),
        ),
        check_vma=False,
    )
```

profile of v0, /device:TPU:2, one launch (start us, length us, event | category | flops | bytes accessed | tf_op | source)
XLA Modules:
  0.0 414.1 jit_solution(1295653864026888875)
XLA Ops:
  8.5 1.8 convolution_bitcast_fusion
  12.2 1.8 copy.118
  14.1 2.3 copy_dynamic-update-slice_fusion
  16.8 15.9 %dynamic-update-slice.7 = f32[6,4,3,4,3,9,128]{6,5,3,1,0,2,4:T(8,128)} dynamic-update-slice(f32[6,4,3,4,3,9,128]{6,5,3,1,0,2,4:T(8,128)} %copy_dynamic-update-slice_fusion, f32[6,4,3,4,3,1,128]{6,5,3,1,0,2,4:T(1,128)S(1)} %copy.120, s32[]{} %constant.354, s32[]{} %constant.354, s32[]{} %constant.354, s32[]{} %constant.354, s32[]{} %constant.354, s32[]{} %constant.355, s32[]{} %constant.354) | dynamic-update-slice | bytes 884740 | tf_op jit(solution)/shard_map/concatenate | solution.py:45
  32.7 3.8 fusion.70
  36.5 1.7 fusion.4
  40.4 2.2 pad_maximum_fusion.1
  42.6 2.5 copy.121
  46.5 1.2 copy-done.1
  48.3 1.5 copy.123
  49.9 1.2 copy-done.4
  59.1 7.7 %collective-permute-start.1 = (bf16[4,8,8,128]{3,2,1,0:T(8,128)(2,1)}, bf16[4,8,8,128]{3,2,1,0:T(8,128)(2,1)}, u32[]{:S(2)}, u32[]{:S(2)}) collective-permute-start(bf16[4,8,8,128]{3,2,1,0:T(8,128)(2,1)} %slice.526), channel_id=1, source_target_pairs={{8,0},{16,8},{24,16},{32,24},{40,32},{48,40},{56,48},{64,56},{72,6... | collective-permute-start | bytes 196616 | tf_op jit(solution)/shard_map/ppermute | solution.py:23
  66.8 2.1 copy.186
  72.1 2.1 collective-permute-start
  80.6 1.2 fusion.68
  81.8 1.2 and_bitcast_fusion.1
  86.0 1.2 compare_and_fusion.1
  87.9 1.8 scatter_fusion.1
  89.7 1.5 copy.125
  91.8 2.4 scatter_fusion.2
  94.2 2.3 copy.126
  96.5 1.1 compare_and_fusion.4
  98.3 1.4 compare_and_fusion.2
  101.5 1.1 bitcast_or_fusion.3
  102.6 1.2 pad_clamp_fusion.2
  103.9 1.6 copy.103
  106.6 1.6 copy.105
  108.2 2.2 gather_fusion.6
  110.4 1.6 fusion.27
  112.0 1.4 gather_fusion.2
  114.2 1.6 maximum_bitcast_fusion.1
  115.8 2.1 gather_fusion.7
  117.9 1.0 fusion.26
  118.9 1.3 maximum_maximum_fusion.1
  120.1 1.3 slice_bitcast_fusion.11
  123.9 1.0 pad_maximum_fusion.15
  125.6 1.3 gather_fusion.5
  127.6 2.1 gather_fusion.1
  132.5 1.0 fusion.28
  134.3 1.3 maximum_maximum_fusion
  138.1 1.0 copy-done.10
  139.8 4.0 convolution_bitcast_fusion.1
  146.0 3.8 scatter-add.66
  149.8 3.8 scatter-add.67
  153.8 1.1 copy.130
  156.0 2.4 fusion.16
  159.0 245.4 %all-reduce.14.cloned.1.call-done = f32[3,3,3,128,128]{4,3,2,1,0:T(8,128)} async-done(((f32[3,3,3,128,128]{4,3,2,1,0:T(8,128)}), f32[3,3,3,128,128]{4,3,2,1,0:T(8,128)}) %all-reduce.14.cloned.1.call-update) | async-done | bytes 1769488 | tf_op jit(solution)/shard_map/psum | solution.py:171
  404.4 2.9 broadcast_multiply_fusion
  (182 shorter events, 48.4 us)
Async XLA Ops:
  7.2 1.4 copy-start
  7.2 397.2 %all-reduce.14.cloned.1.call-start = ((), (), s32[]{:S(2)}) async-start(), calls=%async_computation | async-start | bytes 3538944 | tf_op jit(solution)/shard_map/psum | solution.py:171
  8.5 1.8 copy-start.20
  38.2 0.9 copy-start.22
  38.2 0.9 copy-start.34
  38.2 0.9 copy-start.35
  38.3 0.9 copy-start.36
  38.3 0.9 copy-start.37
  38.3 0.9 copy-start.38
  38.3 0.9 copy-start.39
  39.3 16.9 %copy-start.19 = (s32[6,3]{0,1:T(4,128)}, s32[6,3]{0,1:T(4,128)S(1)}, u32[]{:S(2)}) copy-start(s32[6,3]{0,1:T(4,128)S(1)} %get-tuple-element.88) | copy-start | bytes 220
  40.2 13.6 %copy-start.29 = (pred[6]{0:T(512)(128)(4,1)}, pred[6]{0:T(512)(128)(4,1)S(1)}, u32[]{:S(2)}) copy-start(pred[6]{0:T(512)(128)(4,1)S(1)} %reduce_or.75) | copy-start | bytes 22
  45.1 1.1 copy-start.6
  46.4 1.2 copy-start.1
  49.8 1.3 copy-start.4
  51.2 2.1 copy-start.23
  51.3 3.9 copy-start.30
  52.4 17.5 %copy-start.24 = (pred[6]{0:T(512)(128)(4,1)}, pred[6]{0:T(512)(128)(4,1)S(1)}, u32[]{:S(2)}) copy-start(pred[6]{0:T(512)(128)(4,1)S(1)} %reduce_or.74) | copy-start | bytes 22
  52.5 17.4 %copy-start.31 = (s32[6]{0:T(128)}, s32[6]{0:T(128)S(1)}, u32[]{:S(2)}) copy-start(s32[6]{0:T(128)S(1)} %select_reduce_fusion.4) | copy-start | bytes 76
  59.1 84.8 %collective-permute-start.1 = (bf16[4,8,8,128]{3,2,1,0:T(8,128)(2,1)}, bf16[4,8,8,128]{3,2,1,0:T(8,128)(2,1)}, u32[]{:S(2)}, u32[]{:S(2)}) collective-permute-start(bf16[4,8,8,128]{3,2,1,0:T(8,128)(2,1)} %slice.526), channel_id=1, source_target_pairs={{8,0},{16,8},{24,16},{32,24},{40,32},{48,40},{56,48},{64,56},{72,6... | collective-permute-start | bytes 196616 | tf_op jit(solution)/shard_map/ppermute | solution.py:23
  68.9 1.0 copy-start.2
  69.9 0.7 copy-start.7
  71.4 3.5 copy-start.5
  72.1 50.2 %collective-permute-start = (bf16[4,8,8,128]{3,0,2,1:T(4,128)(2,1)}, bf16[4,8,8,128]{3,0,2,1:T(4,128)(2,1)}, u32[]{:S(2)}, u32[]{:S(2)}) collective-permute-start(bf16[4,8,8,128]{3,0,2,1:T(4,128)(2,1)} %copy.94), channel_id=1, source_target_pairs={{0,8},{8,16},{16,24},{24,32},{32,40},{40,48},{48,56},{56,64},{64,7... | collective-permute-start | bytes 196616 | tf_op jit(solution)/shard_map/ppermute | solution.py:23
  77.0 2.3 copy-start.25
  77.0 6.0 %copy-start.33 = (s32[6,1]{0,1:T(1,128)S(1)}, s32[6,1]{0,1:T(1,128)}, u32[]{:S(2)}) copy-start(s32[6,1]{0,1:T(1,128)} %get-tuple-element.51) | copy-start | bytes 76
  77.0 7.1 %copy-start.3 = (bf16[1,6,8,8,8,128]{5,1,4,3,2,0:T(8,128)(2,1)S(1)}, bf16[1,6,8,8,8,128]{5,1,4,3,2,0:T(8,128)(2,1)}, u32[]{:S(2)}) copy-start(bf16[1,6,8,8,8,128]{5,1,4,3,2,0:T(8,128)(2,1)} %copy-done.2) | copy-start | bytes 2359300
  89.7 1.5 copy-start.41
  89.7 2.1 copy-start.26
  94.2 12.5 %copy-start.40 = (s32[6]{0:T(128)S(1)}, s32[6]{0:T(128)}, u32[]{:S(2)}) copy-start(s32[6]{0:T(128)} %get-tuple-element.66) | copy-start | bytes 76
  118.8 2.6 copy-start.16
  118.9 3.4 copy-start.32
  133.5 2.3 copy-start.8
  133.5 2.3 copy-start.9
  137.4 2.4 copy-start.18
  137.4 2.4 copy-start.21
  138.0 1.0 copy-start.10
  138.0 1.4 copy-start.12
  138.0 1.7 copy-start.14
  143.8 1.6 copy-start.17
  143.8 1.7 copy-start.27
  143.8 1.7 copy-start.28
  153.6 1.3 copy-start.11
  153.6 2.0 copy-start.13
  153.6 2.3 copy-start.15
Sparse Core Ops, SparseCore 0:
  143.9 260.3 all-reduce.13
where the time goes:
time: 416 us; the launch traced here: 414 us
  waiting for transfers between devices  245 us (59%)
  local copies, waits for them, and re-layouts  77.7 us (19%)
  other arithmetic  58.1 us (14%)
  between operations  14.9 us (4%)
  starting transfers between devices  9.9 us (2%)
  matrix products  8.18 us (2%)
    psum x1, waiting for transfers between devices, per_device(): summed = lax.psum(local_grad, ('region', 'group'))  245 us
    concatenate x1, local copies, waits for them, and re-layouts, fold_back(): jnp.concatenate([merged, lax.slice_in_dim(even_rows, 4, 5, 1, which_axis)...  15.9 us
    unnamed x90, local copies, waits for them, and re-layouts  14.1 us
    gather x8, local copies, waits for them, and re-layouts, pick_rows(): gathered = jnp.take(lookup_table, safe_rows, axis=0)  11 us
    ppermute x2, starting transfers between devices, shifted(): return lax.ppermute(block, axis, route)  9.86 us
  transfers between devices with their start and end apart: 3, of which 1 were waited for; matrix products, arithmetic and copies ran while one was open for 21% of the time, Pallas kernels for 0%

commit v1 on v0

--- a/solution.py
+++ b/solution.py
@@ -168,7 +168,7 @@
         jnp.float32
     )
     own_grad = own_grad.at[:, 7].add(pick_rows(returned, (cell_index, in_top)))
-    summed = lax.psum(local_grad, ("region", "group"))
+    summed = lax.psum(lax.psum(local_grad, "group"), "region")
     grad_scale = 1.0 / math.sqrt(
         lax.axis_size("group") * lax.axis_size("region") * block_count * upstream.shape[1] ** 3
     )

time: 416 us -> 316 us (0.76)
  waiting for transfers between devices: 245 us -> 179 us
  other arithmetic: 58.1 us -> 35 us
  local copies, waits for them, and re-layouts: 77.7 us -> 67.8 us
    psum x1 -> x2, waiting for transfers between devices: 245 us -> 179 us  [per_device(): summed = lax.psum(lax.psum(local_grad, 'group'), 'region')]
    gather x8, local copies, waits for them, and re-layouts: 11 us -> 4.51 us  [pick_rows(): gathered = jnp.take(lookup_table, safe_rows, axis=0)]
    unnamed x90 -> x70, local copies, waits for them, and re-layouts: 14.1 us -> 14.6 us
  transfers between devices with their start and end apart: 3 -> 4, of which waited for: 1 -> 2; matrix products, arithmetic and copies ran while one was open for 21% -> 26% of each run, Pallas kernels for 0% -> 0%
where the time goes in v1:
time: 316 us; the launch traced here: 314 us
  waiting for transfers between devices  179 us (57%)
  local copies, waits for them, and re-layouts  67.8 us (21%)
  other arithmetic  35 us (11%)
  between operations  15 us (5%)
  starting transfers between devices  9.74 us (3%)
  matrix products  7.54 us (2%)
    psum x2, waiting for transfers between devices, per_device(): summed = lax.psum(lax.psum(local_grad, 'group'), 'region')  179 us
    concatenate x1, local copies, waits for them, and re-layouts, fold_back(): jnp.concatenate([merged, lax.slice_in_dim(even_rows, 4, 5, 1, which_axis)...  15.7 us
    unnamed x70, local copies, waits for them, and re-layouts  14.6 us
    ppermute x2, starting transfers between devices, shifted(): return lax.ppermute(block, axis, route)  9.66 us
    another operation x6, other arithmetic, fold_back(): jnp.stack([lax.slice_in_dim(even_rows, 0, 4, 1, which_axis), middle_part]...  7.91 us
  transfers between devices with their start and end apart: 4, of which 2 were waited for; matrix products, arithmetic and copies ran while one was open for 26% of the time, Pallas kernels for 0%

profile of v1, /device:TPU:2, one launch (start us, length us, event | category | flops | bytes accessed | tf_op | source)
XLA Modules:
  0.0 314.1 jit_solution(9118897199955358242)
XLA Ops:
  7.2 0.8 copy.188
  9.1 2.1 copy.186
  11.3 0.7 scatter_fusion
  12.1 3.8 %collective-permute-start = (bf16[4,8,8,128]{3,0,2,1:T(4,128)(2,1)S(1)}, bf16[4,8,8,128]{3,0,2,1:T(4,128)(2,1)S(1)}, u32[]{:S(2)}, u32[]{:S(2)}) collective-permute-start(bf16[4,8,8,128]{3,0,2,1:T(4,128)(2,1)S(1)} %copy.94), channel_id=1, source_target_pairs={{0,8},{8,16},{16,24},{24,32},{32,40},{40,48},{48,56},{56,64},{64,7... | collective-permute-start | bytes 196616 | tf_op jit(solution)/shard_map/ppermute | solution.py:23
  15.9 0.9 convolution_bitcast_fusion
  16.9 1.0 slice_bitcast_fusion.2
  18.7 1.8 copy.118
  20.5 2.3 copy_dynamic-update-slice_fusion
  23.3 15.7 %dynamic-update-slice.7 = f32[6,4,3,4,3,9,128]{6,5,3,1,0,2,4:T(8,128)} dynamic-update-slice(f32[6,4,3,4,3,9,128]{6,5,3,1,0,2,4:T(8,128)} %copy_dynamic-update-slice_fusion, f32[6,4,3,4,3,1,128]{6,5,3,1,0,2,4:T(1,128)S(1)} %copy.120, s32[]{} %constant.354, s32[]{} %constant.354, s32[]{} %constant.354, s32[]{} %constant.354, s32[]{} %constant.354, s32[]{} %constant.355, s32[]{} %constant.354) | dynamic-update-slice | bytes 884740 | tf_op jit(solution)/shard_map/concatenate | solution.py:45
  39.0 5.5 %fusion.70 = (f32[6,4,3,4,1,9,128]{6,5,3,1,0,2,4:T(8,128)}, f32[6,4,3,4,9,128]{5,4,3,1,0,2:T(8,128)S(1)}, f32[6,4,3,4,9,128]{5,4,3,1,0,2:T(8,128)S(1)}) fusion(f32[6,4,3,4,3,9,128]{6,5,3,1,0,2,4:T(8,128)} %dynamic-update-slice.7), kind=kLoop, calls=%fused_computation.249 | loop fusion | bytes 7962624 | tf_op jit(solution)/shard_map/slice | solution.py:33
  44.5 1.7 fusion.4
  50.5 2.9 pad_maximum_fusion.1
  53.5 2.5 copy.121
  55.9 3.0 copy.122
  62.6 1.3 slice_bitcast_fusion.11
  66.4 0.7 fusion.35
  67.1 0.7 fusion.37
  67.9 0.7 fusion.28
  68.7 0.8 fusion.40
  71.0 0.7 pad_maximum_fusion.3
  72.3 1.0 copy-done.7
  74.1 4.3 %convolution_bitcast_fusion.1 = f32[3,3,3,128,128]{4,3,2,1,0:T(8,128)} fusion(bf16[6,4,3,4,3,4,1,128]{7,0,6,4,2,5,3,1:T(8,128)(2,1)S(1)} %get-tuple-element.76, bf16[6,4,3,4,3,4,1,128]{7,0,6,4,2,5,3,1:T(8,128)(2,1)S(1)} %get-tuple-element.77, bf16[6,4,3,4,3,4,1,128]{7,0,6,4,2,5,3,1:T(8,128)(2,1)S(1)} %get-tuple-element.75, ...), kind=kOutput, calls=%fused_computation.57 | convolution fusion | flops 342441984 | bytes 4521990 | tf_op jit(solution)/shard_map/nxaybzcf,nxyzo->abcfo/dot_general | solution.py:156
  78.5 2.2 fusion.8
  80.7 1.2 copy-done.2
  82.1 2.2 fusion
  84.3 1.5 copy.123
  86.1 1.1 copy-done.4
  87.2 0.8 scatter_fusion.4
  88.0 0.8 scatter_fusion.5
  88.9 0.8 scatter_fusion.6
  89.8 0.8 scatter_fusion.7
  90.7 5.8 %collective-permute-start.1 = (bf16[4,8,8,128]{3,2,1,0:T(8,128)(2,1)S(1)}, bf16[4,8,8,128]{3,2,1,0:T(8,128)(2,1)S(1)}, u32[]{:S(2)}, u32[]{:S(2)}) collective-permute-start(bf16[4,8,8,128]{3,2,1,0:T(8,128)(2,1)S(1)} %slice.526), channel_id=1, source_target_pairs={{8,0},{16,8},{24,16},{32,24},{40,32},{48,40},{56,48},{64,56},{72,6... | collective-permute-start | bytes 196616 | tf_op jit(solution)/shard_map/ppermute | solution.py:23
  96.6 2.2 copy.124
  98.9 1.7 copy-done.1
  100.8 49.6 %all-reduce.15.cloned.1.call-done = f32[3,3,3,128,128]{4,3,2,1,0:T(8,128)} async-done(((f32[3,3,3,128,128]{4,3,2,1,0:T(8,128)}), f32[3,3,3,128,128]{4,3,2,1,0:T(8,128)}) %all-reduce.15.cloned.1.call-update) | async-done | bytes 1769488 | tf_op jit(solution)/shard_map/psum | solution.py:171
  150.5 0.9 scatter_fusion.1
  151.4 1.5 copy.125
  152.9 1.5 fusion.19
  154.4 2.3 scatter_fusion.2
  156.7 2.3 copy.126
  159.0 0.9 pad_maximum_fusion.16
  160.0 0.8 scatter_fusion.3
  161.9 3.8 %scatter-add.66 = f32[6,8,8,8,128]{4,1,3,2,0:T(8,128)S(1)} dynamic-update-slice(f32[6,8,8,8,128]{4,1,3,2,0:T(8,128)S(1)} %scatter_fusion.3, f32[6,1,8,8,128]{4,1,3,2,0:T(1,128)S(1)} %get-tuple-element.46, s32[]{:T(128)} %constant.164.clone.1, s32[]{:T(128)} %constant.180.clone.1, s32[]{:T(128)} %constant.164.clone.1, s32[]{:T(128)} %constant.164.clone.1, s32[]{:T(128)} %constant.164.clone.1) | dynamic-update-slice | bytes 393220 | tf_op jit(solution)/shard_map/scatter-add | solution.py:166
  165.8 3.8 %scatter-add.67 = f32[6,8,8,8,128]{4,1,3,2,0:T(8,128)S(1)} dynamic-update-slice(f32[6,8,8,8,128]{4,1,3,2,0:T(8,128)S(1)} %scatter-add.66, f32[6,1,8,8,128]{4,1,3,2,0:T(1,128)S(1)} %get-tuple-element.45, s32[]{:T(128)} %constant.164.clone.1, s32[]{:T(128)} %constant.180.clone.1, s32[]{:T(128)} %constant.164.clone.1, s32[]{:T(128)} %constant.164.clone.1, s32[]{:T(128)} %constant.164.clone.1) | dynamic-update-slice | bytes 393220 | tf_op jit(solution)/shard_map/scatter-add | solution.py:170
  169.8 1.1 copy.130
  171.9 2.4 fusion.16
  175.0 129.4 %all-reduce.17.cloned.1.call-done = f32[3,3,3,128,128]{4,3,2,1,0:T(8,128)} async-done(((f32[3,3,3,128,128]{4,3,2,1,0:T(8,128)}), f32[3,3,3,128,128]{4,3,2,1,0:T(8,128)}) %all-reduce.17.cloned.1.call-update) | async-done | bytes 1769488 | tf_op jit(solution)/shard_map/psum | solution.py:171
  304.3 2.9 broadcast_multiply_fusion
  (165 shorter events, 19.6 us)
Async XLA Ops:
  7.2 8.8 %copy-start = (bf16[3,3,3,128,128]{4,3,2,1,0:T(8,128)(2,1)S(1)}, bf16[3,3,3,128,128]{4,3,2,1,0:T(8,128)(2,1)}, u32[]{:S(2)}) copy-start(bf16[3,3,3,128,128]{4,3,2,1,0:T(8,128)(2,1)} %param.22) | copy-start | bytes 2654212
  7.2 8.8 %copy-start.13 = (bf16[1,6,4,4,4,128]{5,4,3,2,1,0:T(4,128)(2,1)S(1)}, bf16[1,6,4,4,4,128]{5,4,3,2,1,0:T(4,128)(2,1)}, u32[]{:S(2)}) copy-start(bf16[1,6,4,4,4,128]{5,4,3,2,1,0:T(4,128)(2,1)} %param.21) | copy-start | bytes 294916
  7.2 143.2 %all-reduce.15.cloned.1.call-start = ((), (), s32[]{:S(2)}) async-start(), calls=%async_computation | async-start | bytes 3538944 | tf_op jit(solution)/shard_map/psum | solution.py:171
  12.1 51.8 %collective-permute-start = (bf16[4,8,8,128]{3,0,2,1:T(4,128)(2,1)S(1)}, bf16[4,8,8,128]{3,0,2,1:T(4,128)(2,1)S(1)}, u32[]{:S(2)}, u32[]{:S(2)}) collective-permute-start(bf16[4,8,8,128]{3,0,2,1:T(4,128)(2,1)S(1)} %copy.94), channel_id=1, source_target_pairs={{0,8},{8,16},{16,24},{24,32},{32,40},{40,48},{48,56},{56,64},{64,7... | collective-permute-start | bytes 196616 | tf_op jit(solution)/shard_map/ppermute | solution.py:23
  46.2 0.7 copy-start.15
  46.2 0.7 copy-start.22
  46.2 0.7 copy-start.23
  46.2 0.7 copy-start.24
  46.2 0.7 copy-start.25
  46.2 0.7 copy-start.26
  46.3 0.7 copy-start.27
  48.2 13.3 %copy-start.16 = (pred[6]{0:T(512)(128)(4,1)}, pred[6]{0:T(512)(128)(4,1)S(1)}, u32[]{:S(2)}) copy-start(pred[6]{0:T(512)(128)(4,1)S(1)} %reduce_or.78) | copy-start | bytes 22
  48.4 11.7 %copy-start.30 = (s32[6]{0:T(128)}, s32[6]{0:T(128)S(1)}, u32[]{:S(2)}) copy-start(s32[6]{0:T(128)S(1)} %get-tuple-element.105) | copy-start | bytes 76
  48.4 11.8 %copy-start.28 = (s32[6]{0:T(128)}, s32[6]{0:T(128)S(1)}, u32[]{:S(2)}) copy-start(s32[6]{0:T(128)S(1)} %get-tuple-element.104) | copy-start | bytes 76
  68.6 1.4 copy-start.5
  68.6 1.4 copy-start.6
  71.7 2.5 copy-start.14
  72.3 1.0 copy-start.7
  72.3 1.5 copy-start.9
  72.3 1.8 copy-start.11
  78.4 225.9 %all-reduce.17.cloned.1.call-start = ((), (), s32[]{:S(2)}) async-start(), calls=%async_computation.1 | async-start | bytes 3538944 | tf_op jit(solution)/shard_map/psum | solution.py:171
  80.6 1.2 copy-start.2
  84.3 2.9 copy-start.21
  85.9 1.3 copy-start.4
  90.7 70.2 %collective-permute-start.1 = (bf16[4,8,8,128]{3,2,1,0:T(8,128)(2,1)S(1)}, bf16[4,8,8,128]{3,2,1,0:T(8,128)(2,1)S(1)}, u32[]{:S(2)}, u32[]{:S(2)}) collective-permute-start(bf16[4,8,8,128]{3,2,1,0:T(8,128)(2,1)S(1)} %slice.526), channel_id=1, source_target_pairs={{8,0},{16,8},{24,16},{32,24},{40,32},{48,40},{56,48},{64,56},{72,6... | collective-permute-start | bytes 196616 | tf_op jit(solution)/shard_map/ppermute | solution.py:23
  96.5 2.3 copy-start.3
  98.8 1.8 copy-start.1
  100.6 49.9 %copy-start.17 = (pred[6]{0:T(512)(128)(4,1)S(1)}, pred[6]{0:T(512)(128)(4,1)}, u32[]{:S(2)}) copy-start(pred[6]{0:T(512)(128)(4,1)} %copy-done.16) | copy-start | bytes 22
  100.6 49.9 %copy-start.31 = (s32[6]{0:T(128)S(1)}, s32[6]{0:T(128)}, u32[]{:S(2)}) copy-start(s32[6]{0:T(128)} %copy-done.30) | copy-start | bytes 76
  152.9 1.5 copy-start.29
  159.0 1.8 copy-start.20
  159.0 2.4 copy-start.18
  159.0 2.4 copy-start.19
  169.6 1.3 copy-start.8
  169.6 1.9 copy-start.10
  169.6 2.3 copy-start.12
Sparse Core Ops, SparseCore 0:
  78.5 71.8 all-reduce.14
  153.9 150.4 all-reduce.16
